TPU v7x, 128 devices: a whole 4x4x4 slice. The times are simulated.
128 devices in a mesh: section: 8 (over y, core), tp: 16 (over x, z).
Axes of the slice: x: 4, y: 4, z: 4, core: 2. Of those that a mesh axis runs over, the one named last changes fastest.
Arguments:
- stream_in: bfloat16 [512, 8192], P(None, 'tp')
- layer_delta: bfloat16 [8, 512, 8192], P('section', None, 'tp')
- norm_gain: float32 [8192], P('tp'), may hold values from 0.25 to 1.75
- out_embed: bfloat16 [8192, 16384], P(None, 'tp')
- exit_blocks: int32 [8, 4], P('section'), may hold values from 0 to 3
- exit_counts: int32 [8], P('section'), may hold values from 1 to 4, 16 in all
- targets: int32 [512], replicated, may hold values from 0 to 16383
Outputs:
- exit_loss: float32 [8, 4, 128], P('section')
Inputs may be any that keep to these rules, and one draw needn't show every extreme that they name: `exit_counts`: each section scores at least one block, the counts of all sections sum to 2 times the number of sections, and some section scores exactly 4. `exit_blocks`: block numbers of the micro-batch's 128-row blocks; only a section's first exit_counts entries are used.
All inputs are finite; a program needn't handle non-finite values.
Results may differ from a plain program's by a relative error of at most 0.02.
Values may be sent and summed in bfloat16 or wider, within the bound.
A program may use at most 128 MiB of HBM per device.

v0:
```python
import jax
import jax.numpy as jnp
from jax import lax
from jax.sharding import PartitionSpec as P

BLK = 128
MAXB = 4
EPS = 1e-05


def prefix(shard, axis, join, neutral):
    place = lax.axis_index(axis)
    gathered = lax.all_gather(shard.astype(jnp.bfloat16), axis)
    state = jnp.zeros_like(shard) + jnp.asarray(neutral, shard.dtype)

    def one(lap, state):
        return join(state, lax.dynamic_index_in_dim(gathered, lap, 0, False).astype(shard.dtype))

    return lax.fori_loop(0, place, one, state)


def from_root(shard, axis, root):
    mine = lax.axis_index(axis) == root
    return lax.psum(jnp.where(mine, shard, jnp.zeros_like(shard)), axis)


def add_terms(first, second):
    return first + second


def row_losses(exit_rows, teach_rows, target_rows, norm_gain, out_embed):
    width = out_embed.shape[0]
    squares = lax.psum(
        (jnp.sum(exit_rows * exit_rows, axis=1), jnp.sum(teach_rows * teach_rows, axis=1)), "tp"
    )
    normed_exit = (
        exit_rows * lax.rsqrt(squares[0] / width + EPS)[:, None] * norm_gain[None, :]
    ).astype(jnp.bfloat16)
    normed_teach = (
        teach_rows * lax.rsqrt(squares[1] / width + EPS)[:, None] * norm_gain[None, :]
    ).astype(jnp.bfloat16)
    vocab_part = out_embed.shape[1]
    logit_exit = jnp.dot(
        lax.all_gather(normed_exit, "tp", axis=1, tiled=True),
        out_embed,
        preferred_element_type=jnp.float32,
    )
    logit_teach = jnp.dot(
        lax.all_gather(normed_teach, "tp", axis=1, tiled=True),
        out_embed,
        preferred_element_type=jnp.float32,
    )
    first_column = lax.axis_index("tp") * vocab_part
    columns = jnp.arange(vocab_part, dtype=jnp.int32)
    hit = (target_rows - first_column)[:, None] == columns[None, :]
    target_part = jnp.sum(jnp.where(hit, logit_exit, 0.0), axis=1)
    peak_exit, peak_teach = lax.pmax(
        (jnp.max(logit_exit, axis=1), jnp.max(logit_teach, axis=1)), "tp"
    )
    weight_teach = jnp.exp(logit_teach - peak_teach[:, None])
    total_exit, total_teach, cross, picked = lax.psum(
        (
            jnp.sum(jnp.exp(logit_exit - peak_exit[:, None]), axis=1),
            jnp.sum(weight_teach, axis=1),
            jnp.sum(weight_teach * (logit_teach - logit_exit), axis=1),
            target_part,
        ),
        "tp",
    )
    log_exit = jnp.log(total_exit) + peak_exit
    log_teach = jnp.log(total_teach) + peak_teach
    return 2.0 * log_exit - picked + cross / total_teach - log_teach


def body(stream_in, layer_delta, norm_gain, out_embed, exit_blocks, exit_counts, targets):
    stream = stream_in.astype(jnp.float32)
    mine_delta = layer_delta[0].astype(jnp.float32)
    before = prefix(mine_delta, "section", add_terms, jnp.zeros_like(mine_delta))
    exit_all = stream + before + mine_delta
    final_all = from_root(
        exit_all.astype(jnp.bfloat16), "section", lax.axis_size("section") - 1
    ).astype(exit_all.dtype)
    starts = [exit_blocks[0, slot_index] * BLK for slot_index in range(MAXB)]
    exit_rows = jnp.concatenate(
        [lax.dynamic_slice_in_dim(exit_all, start, BLK, 0) for start in starts], axis=0
    )
    teach_rows = jnp.concatenate(
        [lax.dynamic_slice_in_dim(final_all, start, BLK, 0) for start in starts], axis=0
    )
    target_rows = jnp.concatenate(
        [lax.dynamic_slice_in_dim(targets, start, BLK, 0) for start in starts], axis=0
    )
    losses = row_losses(exit_rows, teach_rows, target_rows, norm_gain, out_embed).reshape(MAXB, BLK)
    keep = jnp.arange(MAXB, dtype=jnp.int32) < exit_counts[0]
    return jnp.where(keep[:, None], losses, 0.0)[None]


def solution(mesh):
    placed = (
        P(None, "tp"),
        P("section", None, "tp"),
        P("tp"),
        P(None, "tp"),
        P("section", None),
        P("section"),
        P(),
    )
    return jax.shard_map(
        body, mesh=mesh, in_specs=placed, out_specs=P("section", None, None), check_vma=False
    )
```

profile of v0, /device:TPU:0, one launch (start us, length us, event | category | flops | bytes accessed | tf_op | source)
XLA Modules:
  0.0 407.7 jit_solution(8671719075948042999)
XLA Ops:
  6.5 0.7 all-gather.4.cloned.1.call-update
  7.3 0.0 all-reduce.5.cloned.1.call-start
  7.3 36.3 %all-gather.4.cloned.1.call-done = bf16[8,512,512]{2,1,0:T(8,128)(2,1)} async-done(((bf16[1,512,512]{2,1,0:T(8,128)(2,1)}), bf16[8,512,512]{2,1,0:T(8,128)(2,1)}) %all-gather.4.cloned.1.call-update) | async-done | bytes 4194320 | tf_op jit(solution)/shard_map/all_gather | solution.py:13
  43.6 0.1 broadcast_in_dim.21
  43.8 0.0 copy-start
  43.8 1.0 copy-done
  44.8 0.3 copy-done.1
  45.1 1.1 convert_select_fusion
  46.2 0.0 all-reduce.5.cloned.1.call-update
  46.2 0.0 all-gather.8.cloned.1.call-start
  46.2 0.7 fusion.3
  49.5 0.1 constant_dynamic-slice_fusion.7
  49.6 0.1 multiply_reduce_fusion.2
  49.8 0.0 copy-start.4
  49.8 64.8 %all-reduce.5.cloned.1.call-done = bf16[512,512]{1,0:T(8,128)(2,1)} async-done(((bf16[512,512]{1,0:T(8,128)(2,1)}), bf16[512,512]{1,0:T(8,128)(2,1)}) %all-reduce.5.cloned.1.call-update) | async-done | bytes 524304 | tf_op jit(solution)/shard_map/psum | solution.py:24
  114.6 1.2 convert_element_type.33
  115.8 0.1 constant_dynamic-slice_fusion.3
  115.9 0.2 multiply_reduce_fusion.1
  116.0 40.5 %all-reduce.1 = (f32[512]{0:T(512)S(1)}, f32[512]{0:T(512)S(1)}) all-reduce(f32[512]{0:T(512)S(1)} %multiply_reduce_fusion.1, f32[512]{0:T(512)S(1)} %multiply_reduce_fusion.2), channel_id=1, replica_groups=mesh['section'=8,'tp'=16] {'tp'}, use_global_device_ids=true, to_apply=%region_12.13 | all-reduce | flops 1024 | bytes 8192 | tf_op jit(solution)/shard_map/psum | solution.py:33
  156.6 1.3 multiply_convert_fusion.1
  157.8 0.0 all-gather.8.cloned.1.call-update
  157.9 0.0 all-gather.6.cloned.1.call-start
  157.9 0.5 all-gather.6.cloned.1.call-update
  159.1 0.1 fusion.2
  159.2 69.9 %all-gather.8.cloned.1.call-done = bf16[512,8192]{1,0:T(8,128)(2,1)} async-done(((bf16[512,512]{1,0:T(8,128)(2,1)}), bf16[512,8192]{1,0:T(8,128)(2,1)}) %all-gather.8.cloned.1.call-update) | async-done | bytes 8388624 | tf_op jit(solution)/shard_map/all_gather | solution.py:49
  229.1 14.8 %fusion.4 = (f32[512]{0:T(512)S(1)}, f32[512,1024]{1,0:T(8,128)S(1)}) fusion(bf16[512,8192]{1,0:T(8,128)(2,1)} %all-gather.8.cloned.1.call-done, bf16[8192,1024]{1,0:T(8,128)(2,1)} %param.12), kind=kOutput, calls=%fused_computation.31 | convolution fusion | flops 8590458880 | bytes 27265024 | tf_op jit(solution)/shard_map/dot_general | solution.py:48
  243.9 63.8 %all-gather.6.cloned.1.call-done = bf16[512,8192]{1,0:T(8,128)(2,1)} async-done(((bf16[512,512]{1,0:T(8,128)(2,1)}), bf16[512,8192]{1,0:T(8,128)(2,1)}) %all-gather.6.cloned.1.call-update) | async-done | bytes 8388624 | tf_op jit(solution)/shard_map/all_gather | solution.py:44
  307.7 16.0 %fusion.1 = (f32[512]{0:T(512)S(1)}, f32[512]{0:T(512)S(1)}, f32[512,1024]{1,0:T(8,128)}) fusion(s32[512]{0:T(512)S(1)} %add_subtract_fusion, bf16[512,8192]{1,0:T(8,128)(2,1)} %all-gather.6.cloned.1.call-done, bf16[8192,1024]{1,0:T(8,128)(2,1)} %param.12), kind=kOutput, calls=%fused_computation.28 | convolution fusion | flops 8592031744 | bytes 27269120 | tf_op jit(solution)/shard_map/dot_general | solution.py:43
  323.7 38.1 %all-reduce.2 = (f32[512]{0:T(512)S(1)}, f32[512]{0:T(512)S(1)}) all-reduce(f32[512]{0:T(512)S(1)} %get-tuple-element.70, f32[512]{0:T(512)S(1)} %get-tuple-element.32), channel_id=1, replica_groups=mesh['section'=8,'tp'=16] {'tp'}, use_global_device_ids=true, to_apply=%region_14.15 | all-reduce | flops 1024 | bytes 8192 | tf_op jit(solution)/shard_map/pmax | solution.py:57
  361.8 2.7 multiply_reduce_fusion
  364.5 35.9 %all-reduce = (f32[512]{0:T(512)S(1)}, f32[512]{0:T(512)S(1)}, f32[512]{0:T(512)S(1)}, f32[512]{0:T(512)S(1)}) all-reduce(f32[512]{0:T(512)S(1)} %get-tuple-element.30, f32[512]{0:T(512)S(1)} %get-tuple-element.29, f32[512]{0:T(512)S(1)} %get-tuple-element.33, f32[512]{0:T(512)S(1)} %get-tuple-element.31), channel_id=1, replica_groups=mesh['section'=8,'tp'=16] {'tp'}, use_global_device_ids=true, to_apply=%region_18.19 | all-reduce | flops 2048 | bytes 16384 | tf_op jit(solution)/shard_map/psum | solution.py:61
  400.5 0.7 bitcast_select_fusion
  (11 shorter events, 0.1 us)
Async XLA Ops:
  6.5 37.1 %all-gather.4.cloned.1.call-start = ((), (), s32[]{:S(2)}) async-start(), calls=%async_computation | async-start | bytes 4718592 | tf_op jit(solution)/shard_map/all_gather | solution.py:13
  7.3 107.4 %all-reduce.5.cloned.1.call-start = ((), (), s32[]{:S(2)}) async-start(), calls=%async_computation.2 | async-start | bytes 1048576 | tf_op jit(solution)/shard_map/psum | solution.py:24
  43.8 1.0 copy-start
  43.8 1.3 copy-start.1
  45.1 1.1 copy-start.2
  46.2 182.9 %all-gather.8.cloned.1.call-start = ((), (), s32[]{:S(2)}) async-start(), calls=%async_computation.3 | async-start | bytes 8912896 | tf_op jit(solution)/shard_map/all_gather | solution.py:49
  49.8 106.8 %copy-start.4 = (f32[512]{0:T(512)S(1)}, f32[512]{0:T(512)}, u32[]{:S(2)}) copy-start(f32[512]{0:T(512)} %param.11) | copy-start | bytes 6148
  156.6 2.5 copy-start.3
  157.9 149.8 %all-gather.6.cloned.1.call-start = ((), (), s32[]{:S(2)}) async-start(), calls=%async_computation.1 | async-start | bytes 8912896 | tf_op jit(solution)/shard_map/all_gather | solution.py:44
Sparse Core Ops, SparseCore 0:
  9.0 34.5 all-gather.3
  46.3 68.2 all-reduce.4
  158.0 71.0 all-gather.7
  231.1 76.6 all-gather.5
where the time goes:
time: 408 us
  waiting for transfers between devices  236 us (58%)
  blocking collectives  115 us (28%)
  matrix products  30.8 us (8%)
  between operations  16.5 us (4%)
  other arithmetic  7.16 us (2%)
    all_gather x1, waiting for transfers between devices, row_losses(): lax.all_gather(normed_teach, 'tp', axis=1, tiled=True)  69.9 us
    psum x1, waiting for transfers between devices, from_root(): return lax.psum(jnp.where(mine, shard, jnp.zeros_like(shard)), axis)  64.8 us
    all_gather x1, waiting for transfers between devices, row_losses(): lax.all_gather(normed_exit, 'tp', axis=1, tiled=True)  63.8 us
    psum x1, blocking collectives, row_losses(): lax.psum((jnp.sum(exit_rows * exit_rows, axis=1), jnp.sum(teach_rows * te...  40.5 us
    pmax x1, blocking collectives, row_losses(): lax.pmax((jnp.max(logit_exit, axis=1), jnp.max(logit_teach, axis=1)), 'tp')  38.1 us
    all_gather x1, waiting for transfers between devices, prefix(): gathered = lax.all_gather(shard.astype(jnp.bfloat16), axis)  36.3 us
    psum x1, blocking collectives, row_losses(): lax.psum((jnp.sum(jnp.exp(logit_exit - peak_exit[:, None]), axis=1), jnp....  35.9 us
    dot_general x1, matrix products, row_losses(): jnp.dot(lax.all_gather(normed_exit, 'tp', axis=1, tiled=True), out_embed,...  16 us
  transfers between devices with their start and end apart: 4, of which 4 were waited for; matrix products, arithmetic and copies ran while one was open for 4% of the time, Pallas kernels for 0%

commit v1 on v0

--- a/solution.py
+++ b/solution.py
@@ -6,6 +6,12 @@
 BLK = 128
 MAXB = 4
 EPS = 1e-05
+
+
+def gather_and_add(x, axis):
+    terms = lax.all_gather(x, axis, axis=0, tiled=False)
+    total = terms.sum(axis=0)
+    return total
 
 
 def prefix(shard, axis, join, neutral):
@@ -21,7 +27,7 @@
 
 def from_root(shard, axis, root):
     mine = lax.axis_index(axis) == root
-    return lax.psum(jnp.where(mine, shard, jnp.zeros_like(shard)), axis)
+    return gather_and_add(jnp.where(mine, shard, jnp.zeros_like(shard)), axis)
 
 
 def add_terms(first, second):

time: 408 us -> 382 us (0.936)
  waiting for transfers between devices: 236 us -> 208 us
    psum x1 -> x0, waiting for transfers between devices: 64.8 us -> none  [from_root(): return lax.psum(jnp.where(mine, shard, jnp.zeros_like(shard)), axis)]
    all_gather x0 -> x1, waiting for transfers between devices: none -> 36 us  [gather_and_add(): terms = lax.all_gather(x, axis, axis=0, tiled=False)]
where the time goes in v1:
time: 382 us
  waiting for transfers between devices  208 us (54%)
  blocking collectives  115 us (30%)
  matrix products  30.8 us (8%)
  between operations  16.4 us (4%)
  other arithmetic  9.18 us (2%)
    all_gather x1, waiting for transfers between devices, row_losses(): lax.all_gather(normed_teach, 'tp', axis=1, tiled=True)  71.1 us
    all_gather x1, waiting for transfers between devices, row_losses(): lax.all_gather(normed_exit, 'tp', axis=1, tiled=True)  63.8 us
    psum x1, blocking collectives, row_losses(): lax.psum((jnp.sum(exit_rows * exit_rows, axis=1), jnp.sum(teach_rows * te...  40.5 us
    pmax x1, blocking collectives, row_losses(): lax.pmax((jnp.max(logit_exit, axis=1), jnp.max(logit_teach, axis=1)), 'tp')  38.1 us
    all_gather x1, waiting for transfers between devices, prefix(): gathered = lax.all_gather(shard.astype(jnp.bfloat16), axis)  36.3 us
    all_gather x1, waiting for transfers between devices, gather_and_add(): terms = lax.all_gather(x, axis, axis=0, tiled=False)  36 us
    psum x1, blocking collectives, row_losses(): lax.psum((jnp.sum(jnp.exp(logit_exit - peak_exit[:, None]), axis=1), jnp....  35.9 us
    dot_general x1, matrix products, row_losses(): jnp.dot(lax.all_gather(normed_exit, 'tp', axis=1, tiled=True), out_embed,...  16 us
  transfers between devices with their start and end apart: 4, of which 4 were waited for; matrix products, arithmetic and copies ran while one was open for 4% of the time, Pallas kernels for 0%

profile of v1, /device:TPU:0, one launch (start us, length us, event | category | flops | bytes accessed | tf_op | source)
XLA Modules:
  0.0 381.9 jit_solution(7774481835155439892)
XLA Ops:
  6.5 0.7 all-gather.6.cloned.1.call-update
  7.3 0.0 all-gather.12.cloned.1.call-start
  7.3 36.3 %all-gather.6.cloned.1.call-done = bf16[8,512,512]{2,1,0:T(8,128)(2,1)} async-done(((bf16[1,512,512]{2,1,0:T(8,128)(2,1)}), bf16[8,512,512]{2,1,0:T(8,128)(2,1)}) %all-gather.6.cloned.1.call-update) | async-done | bytes 4194320 | tf_op jit(solution)/shard_map/all_gather | solution.py:19
  43.6 0.1 broadcast_in_dim.21
  43.8 1.0 copy-done
  44.8 0.3 copy-done.1
  45.1 1.0 convert_select_fusion
  46.1 0.0 all-gather.12.cloned.1.call-update
  46.2 0.0 all-gather.10.cloned.1.call-start
  46.2 0.6 fusion.3
  49.3 0.1 constant_dynamic-slice_fusion.7
  49.4 0.2 multiply_reduce_fusion.2
  49.6 36.0 %all-gather.12.cloned.1.call-done = bf16[4096,512]{1,0:T(8,128)(2,1)} async-done(((bf16[512,512]{1,0:T(8,128)(2,1)}), bf16[4096,512]{1,0:T(8,128)(2,1)}) %all-gather.12.cloned.1.call-update) | async-done | bytes 4194320 | tf_op jit(solution)/shard_map/all_gather | solution.py:12
  85.6 3.1 reduce_sum.69
  88.7 0.0 copy-start.3
  88.7 0.1 convert_element_type.35
  88.8 0.1 constant_dynamic-slice_fusion.3
  88.9 0.2 multiply_reduce_fusion.1
  89.1 40.5 %all-reduce.1 = (f32[512]{0:T(512)S(1)}, f32[512]{0:T(512)S(1)}) all-reduce(f32[512]{0:T(512)S(1)} %multiply_reduce_fusion.1, f32[512]{0:T(512)S(1)} %multiply_reduce_fusion.2), channel_id=1, replica_groups=mesh['section'=8,'tp'=16] {'tp'}, use_global_device_ids=true, to_apply=%region_12.13 | all-reduce | flops 1024 | bytes 8192 | tf_op jit(solution)/shard_map/psum | solution.py:39
  129.6 1.3 multiply_convert_fusion.1
  130.9 0.0 all-gather.10.cloned.1.call-update
  130.9 0.0 all-gather.8.cloned.1.call-start
  130.9 0.5 all-gather.8.cloned.1.call-update
  132.1 0.1 fusion.2
  132.2 71.1 %all-gather.10.cloned.1.call-done = bf16[512,8192]{1,0:T(8,128)(2,1)} async-done(((bf16[512,512]{1,0:T(8,128)(2,1)}), bf16[512,8192]{1,0:T(8,128)(2,1)}) %all-gather.10.cloned.1.call-update) | async-done | bytes 8388624 | tf_op jit(solution)/shard_map/all_gather | solution.py:55
  203.3 14.8 %fusion.4 = (f32[512]{0:T(512)S(1)}, f32[512,1024]{1,0:T(8,128)S(1)}) fusion(bf16[512,8192]{1,0:T(8,128)(2,1)} %all-gather.10.cloned.1.call-done, bf16[8192,1024]{1,0:T(8,128)(2,1)} %param.12), kind=kOutput, calls=%fused_computation.31 | convolution fusion | flops 8590458880 | bytes 27265024 | tf_op jit(solution)/shard_map/dot_general | solution.py:54
  218.2 63.8 %all-gather.8.cloned.1.call-done = bf16[512,8192]{1,0:T(8,128)(2,1)} async-done(((bf16[512,512]{1,0:T(8,128)(2,1)}), bf16[512,8192]{1,0:T(8,128)(2,1)}) %all-gather.8.cloned.1.call-update) | async-done | bytes 8388624 | tf_op jit(solution)/shard_map/all_gather | solution.py:50
  281.9 16.0 %fusion.1 = (f32[512]{0:T(512)S(1)}, f32[512]{0:T(512)S(1)}, f32[512,1024]{1,0:T(8,128)}) fusion(s32[512]{0:T(512)S(1)} %add_subtract_fusion, bf16[512,8192]{1,0:T(8,128)(2,1)} %all-gather.8.cloned.1.call-done, bf16[8192,1024]{1,0:T(8,128)(2,1)} %param.12), kind=kOutput, calls=%fused_computation.28 | convolution fusion | flops 8592031744 | bytes 27269120 | tf_op jit(solution)/shard_map/dot_general | solution.py:49
  297.9 38.1 %all-reduce.2 = (f32[512]{0:T(512)S(1)}, f32[512]{0:T(512)S(1)}) all-reduce(f32[512]{0:T(512)S(1)} %get-tuple-element.70, f32[512]{0:T(512)S(1)} %get-tuple-element.32), channel_id=1, replica_groups=mesh['section'=8,'tp'=16] {'tp'}, use_global_device_ids=true, to_apply=%region_14.15 | all-reduce | flops 1024 | bytes 8192 | tf_op jit(solution)/shard_map/pmax | solution.py:63
  336.1 2.7 multiply_reduce_fusion
  338.8 35.9 %all-reduce = (f32[512]{0:T(512)S(1)}, f32[512]{0:T(512)S(1)}, f32[512]{0:T(512)S(1)}, f32[512]{0:T(512)S(1)}) all-reduce(f32[512]{0:T(512)S(1)} %get-tuple-element.30, f32[512]{0:T(512)S(1)} %get-tuple-element.29, f32[512]{0:T(512)S(1)} %get-tuple-element.33, f32[512]{0:T(512)S(1)} %get-tuple-element.31), channel_id=1, replica_groups=mesh['section'=8,'tp'=16] {'tp'}, use_global_device_ids=true, to_apply=%region_18.19 | all-reduce | flops 2048 | bytes 16384 | tf_op jit(solution)/shard_map/psum | solution.py:67
  374.7 0.7 bitcast_select_fusion
  (12 shorter events, 0.1 us)
Async XLA Ops:
  6.5 37.1 %all-gather.6.cloned.1.call-start = ((), (), s32[]{:S(2)}) async-start(), calls=%async_computation | async-start | bytes 4718592 | tf_op jit(solution)/shard_map/all_gather | solution.py:19
  7.3 78.3 %all-gather.12.cloned.1.call-start = ((), (), s32[]{:S(2)}) async-start(), calls=%async_computation.3 | async-start | bytes 4718592 | tf_op jit(solution)/shard_map/all_gather | solution.py:12
  43.8 1.0 copy-start
  43.8 1.3 copy-start.1
  43.8 2.4 copy-start.2
  46.2 157.2 %all-gather.10.cloned.1.call-start = ((), (), s32[]{:S(2)}) async-start(), calls=%async_computation.2 | async-start | bytes 8912896 | tf_op jit(solution)/shard_map/all_gather | solution.py:55
  85.6 44.0 %copy-start.4 = (f32[512]{0:T(512)S(1)}, f32[512]{0:T(512)}, u32[]{:S(2)}) copy-start(f32[512]{0:T(512)} %param.11) | copy-start | bytes 6148
  88.7 43.5 %copy-start.3 = (s32[512]{0:T(512)S(1)}, s32[512]{0:T(512)}, u32[]{:S(2)}) copy-start(s32[512]{0:T(512)} %param.15) | copy-start | bytes 6148
  130.9 151.1 %all-gather.8.cloned.1.call-start = ((), (), s32[]{:S(2)}) async-start(), calls=%async_computation.1 | async-start | bytes 8912896 | tf_op jit(solution)/shard_map/all_gather | solution.py:50
Sparse Core Ops, SparseCore 0:
  9.0 34.5 all-gather.5
  46.3 39.2 all-gather.11
  131.0 72.2 all-gather.9
  205.3 76.6 all-gather.7
